TPU v7x, 512 devices: a whole 4x8x8 slice. The times are simulated.
512 devices in a mesh: dp: 64 (over z_hi, x, y), tile: 8 (over z_lo, core).
Axes of the slice: x: 4, y: 8, z: 8 (z_hi: 2, z_lo: 4; z = z_hi * 4 + z_lo), core: 2. Of those that a mesh axis runs over, the one named last changes fastest.
Arguments:
- feats: bfloat16 [4096, 2048], P('dp'), may hold values from -11 to 11
- jitter: bfloat16 [4096, 2048], P('dp'), may hold values from -1.5 to 1.5
- mask_ids: int32 [4096, 2], P('dp'), may hold values from 0 to 31
- proj_weight: bfloat16 [2048, 4096], P('dp', 'tile'), may hold values from -0.125 to 0.125
Outputs:
- feats_grad: float32 [4096, 2048], P('dp', 'tile')
- diag_corr: float32 [4096], P('tile')
- cross_power: float32 [], replicated
All inputs are finite; a program needn't handle non-finite values.
Results may differ from a plain program's by a relative error of at most 0.02.
Values may be sent and summed in bfloat16 or wider, within the bound.
No kernel may reach another device: no remote copies, remote signals or barrier semaphores. Data moves between devices by JAX's collectives and lax.ppermute only.
A program may use at most 64 MiB of HBM per device.

v0:
```python
import jax
import jax.numpy as jnp
from jax import lax
from jax.sharding import PartitionSpec as P

EMB = 4096
GROUPS = 32
LAMBDA_OFF = 0.0051
NORM_EPS = 1e-05
LOSS_SCALE = 65536.0


def masked_views(feats, jitter, mask_ids):
    width = feats.shape[1]
    group_size = width // GROUPS
    channel_group = lax.broadcasted_iota(jnp.int32, (1, width), 1) // group_size
    keep_a = (channel_group != mask_ids[:, 0:1]).astype(jnp.float32)
    keep_b = (channel_group != mask_ids[:, 1:2]).astype(jnp.float32)
    values = feats.astype(jnp.float32)
    view_a = (values * keep_a).astype(jnp.bfloat16)
    view_b = (values * keep_b + jitter.astype(jnp.float32)).astype(jnp.bfloat16)
    return (view_a, view_b, keep_a, keep_b)


def contract_last(left, right):
    return lax.dot_general(
        left, right, (((1,), (1,)), ((), ())), preferred_element_type=jnp.float32
    )


def on_device(feats, jitter, mask_ids, proj_weight):
    view_a, view_b, keep_a, keep_b = masked_views(feats, jitter, mask_ids)
    rows = feats.shape[0]
    total = rows * lax.axis_size("dp")
    piece = lax.all_gather(proj_weight, "dp", axis=0, tiled=True)
    raw_a = jnp.dot(view_a, piece, preferred_element_type=jnp.float32)
    raw_b = jnp.dot(view_b, piece, preferred_element_type=jnp.float32)
    raw_a = raw_a.astype(jnp.bfloat16)
    raw_b = raw_b.astype(jnp.bfloat16)
    values_a = raw_a.astype(jnp.float32)
    values_b = raw_b.astype(jnp.float32)
    moment_sums = lax.psum(
        (
            jnp.sum(values_a, axis=0),
            jnp.sum(values_a * values_a, axis=0),
            jnp.sum(values_b, axis=0),
            jnp.sum(values_b * values_b, axis=0),
        ),
        "dp",
    )
    mean_a = moment_sums[0] / total
    mean_b = moment_sums[2] / total
    inv_a = lax.rsqrt(moment_sums[1] / total - mean_a * mean_a + NORM_EPS)
    inv_b = lax.rsqrt(moment_sums[3] / total - mean_b * mean_b + NORM_EPS)
    norm_a = ((values_a - mean_a) * inv_a).astype(jnp.bfloat16)
    norm_b = ((values_b - mean_b) * inv_b).astype(jnp.bfloat16)
    outgoing_a, outgoing_b = (norm_a, norm_b)
    gathered_a, gathered_b = (
        lax.all_gather(outgoing_a, "dp", axis=0, tiled=True),
        lax.all_gather(outgoing_b, "dp", axis=0, tiled=True),
    )
    whole_a, whole_b = (gathered_a, gathered_b)
    za = norm_a.astype(jnp.float32)
    zb = norm_b.astype(jnp.float32)
    diag_corr = jnp.sum(whole_a.astype(jnp.float32) * whole_b.astype(jnp.float32), axis=0) / total
    gram_a, gram_b = (
        lax.psum(contract_last(norm_a, whole_a).astype(jnp.bfloat16), "tile").astype(jnp.float32),
        lax.psum(contract_last(norm_b, whole_b).astype(jnp.bfloat16), "tile").astype(jnp.float32),
    )
    trace_part = jnp.sum(gram_a * gram_b)
    gram_bf_a = gram_a.astype(jnp.bfloat16)
    gram_bf_b = gram_b.astype(jnp.bfloat16)
    coeff = -2.0 * (1.0 - diag_corr) - 2.0 * LAMBDA_OFF * diag_corr
    factor = 2.0 * LAMBDA_OFF / (total * total)
    grad_na = zb * coeff / total + factor * jnp.dot(
        gram_bf_b, whole_a, preferred_element_type=jnp.float32
    )
    grad_nb = za * coeff / total + factor * jnp.dot(
        gram_bf_a, whole_b, preferred_element_type=jnp.float32
    )
    sums = lax.psum(
        (
            jnp.sum(grad_na, axis=0),
            jnp.sum(grad_na * za, axis=0),
            jnp.sum(grad_nb, axis=0),
            jnp.sum(grad_nb * zb, axis=0),
            trace_part,
        ),
        "dp",
    )
    dz_a = (inv_a * (grad_na - sums[0] / total - za * (sums[1] / total))).astype(jnp.bfloat16)
    dz_b = (inv_b * (grad_nb - sums[2] / total - zb * (sums[3] / total))).astype(jnp.bfloat16)
    cross_power = sums[4] / (total * total) / EMB
    piece = lax.all_gather(proj_weight, "dp", axis=0, tiled=True)
    combined = keep_a * contract_last(dz_a, piece) + keep_b * contract_last(dz_b, piece)
    feats_grad = LOSS_SCALE * lax.psum_scatter(
        combined.astype(jnp.bfloat16), "tile", scatter_dimension=1, tiled=True
    ).astype(jnp.float32)
    return (feats_grad, diag_corr, cross_power)


def solution(mesh):
    in_specs = (P("dp", None), P("dp", None), P("dp", None), P("dp", "tile"))
    out_specs = (P("dp", "tile"), P("tile"), P())
    return jax.shard_map(
        on_device, mesh=mesh, in_specs=in_specs, out_specs=out_specs, check_vma=False
    )
```

profile of v0, /device:TPU:2, one launch (start us, length us, event | category | flops | bytes accessed | tf_op | source)
XLA Modules:
  0.0 1044.2 jit_solution(3339325027411994053)
XLA Ops:
  7.2 0.0 all-gather.4.cloned.1.call-start
  7.2 0.7 all-gather.4.cloned.1.call-update
  7.9 0.0 all-gather.6.cloned.1.call-start
  8.0 0.8 slice_bitcast_fusion
  8.7 147.5 %all-gather.4.cloned.1.call-done = bf16[2048,512]{1,0:T(8,128)(2,1)} async-done(((bf16[32,512]{1,0:T(8,128)(2,1)}), bf16[2048,512]{1,0:T(8,128)(2,1)}) %all-gather.4.cloned.1.call-update) | async-done | bytes 2097168 | tf_op jit(solution)/shard_map/all_gather | solution.py:35
  156.2 2.2 multiply_reduce_fusion.3
  158.5 2.3 fusion.42
  160.8 186.2 %all-reduce.1 = (f32[512]{0:T(512)S(1)}, f32[512]{0:T(512)S(1)}, f32[512]{0:T(512)S(1)}, f32[512]{0:T(512)S(1)}) all-reduce(f32[512]{0:T(512)S(1)} %get-tuple-element.10, f32[512]{0:T(512)S(1)} %get-tuple-element.9, f32[512]{0:T(512)S(1)} %get-tuple-element.8, f32[512]{0:T(512)S(1)} %get-tuple-element.7), channel_id=1, replica_groups=mesh['dp'=64,'tile'=8] {'dp'}, use_global_device_ids=true, to_apply=%region_3.4 | all-reduce | flops 2048 | bytes 16384 | tf_op jit(solution)/shard_map/psum | solution.py:42
  347.0 0.6 multiply_convert_fusion
  347.6 0.0 all-gather.6.cloned.1.call-update
  347.6 0.0 all-gather.8.cloned.1.call-start
  347.7 0.6 multiply_convert_fusion.1
  348.3 0.0 copy-start.3
  348.3 0.0 all-gather.8.cloned.1.call-update
  348.4 0.0 all-reduce.5.cloned.1.call-start
  348.4 186.0 %all-gather.6.cloned.1.call-done = bf16[4096,512]{1,0:T(8,128)(2,1)} async-done(((bf16[64,512]{1,0:T(8,128)(2,1)}), bf16[4096,512]{1,0:T(8,128)(2,1)}) %all-gather.6.cloned.1.call-update) | async-done | bytes 4194320 | tf_op jit(solution)/shard_map/all_gather | solution.py:59
  534.4 4.4 convolution_convert_fusion
  538.8 152.4 %all-gather.8.cloned.1.call-done = bf16[4096,512]{1,0:T(8,128)(2,1)} async-done(((bf16[64,512]{1,0:T(8,128)(2,1)}), bf16[4096,512]{1,0:T(8,128)(2,1)}) %all-gather.8.cloned.1.call-update) | async-done | bytes 4194320 | tf_op jit(solution)/shard_map/all_gather | solution.py:60
  691.2 0.0 copy-done.3
  691.2 4.4 convolution_convert_fusion.1
  695.6 0.0 all-reduce.5.cloned.1.call-update
  695.6 0.0 copy-start.2
  695.6 0.0 reduce-scatter.2.cloned.1.call-start
  695.6 4.6 multiply_reduce_fusion
  700.3 0.6 multiply_subtract_fusion
  700.8 68.8 %all-reduce.5.cloned.1.call-done = (bf16[64,4096]{1,0:T(8,128)(2,1)}, bf16[64,4096]{1,0:T(8,128)(2,1)}) async-done(((bf16[64,4096]{1,0:T(8,128)(2,1)}, bf16[64,4096]{1,0:T(8,128)(2,1)}), (bf16[64,4096]{1,0:T(8,128)(2,1)}, bf16[64,4096]{1,0:T(8,128)(2,1)})) %all-reduce.5.cloned.1.call-update) | async-done | bytes 1048592 | tf_op jit(solution)/shard_map/psum | solution.py:68
  769.7 0.0 copy-start
  769.7 0.0 copy-start.4
  769.7 2.2 multiply_reduce_fusion.1
  771.9 0.0 copy-done.2
  771.9 0.0 copy-start.1
  771.9 3.4 fusion.40
  775.3 0.0 copy-done
  775.3 0.0 copy-done.4
  775.3 0.9 fusion.41
  776.2 196.4 %all-reduce = (f32[512]{0:T(512)S(1)}, f32[512]{0:T(512)S(1)}, f32[512]{0:T(512)S(1)}, f32[512]{0:T(512)S(1)}, f32[]{:T(128)}) all-reduce(f32[512]{0:T(512)S(1)} %get-tuple-element.6, f32[512]{0:T(512)S(1)} %get-tuple-element.5, f32[512]{0:T(512)S(1)} %get-tuple-element.4, ...), channel_id=1, replica_groups=mesh['dp'=64,'tile'=8] {'dp'}, use_global_device_ids=true, to_apply=%region_13.14 | all-reduce | flops 2049 | bytes 16392 | tf_op jit(solution)/shard_map/psum | solution.py:81
  972.6 0.0 copy-done.1
  972.6 0.8 convolution_select_fusion.1
  973.3 1.5 fusion.1
  974.8 0.0 reduce-scatter.2.cloned.1.call-update
  975.4 59.7 %reduce-scatter.2.cloned.1.call-done = bf16[64,256]{1,0:T(8,128)(2,1)} async-done(((bf16[64,2048]{1,0:T(8,128)(2,1)}), bf16[64,256]{1,0:T(8,128)(2,1)}) %reduce-scatter.2.cloned.1.call-update) | async-done | bytes 32784 | tf_op jit(solution)/shard_map/reduce_scatter | solution.py:96
  1035.1 1.4 convert_multiply_fusion.6
  (5 shorter events, 0.0 us)
Async XLA Ops:
  7.2 149.1 %all-gather.4.cloned.1.call-start = ((), (), s32[]{:S(2)}) async-start(), calls=%async_computation.1 | async-start | bytes 2129920 | tf_op jit(solution)/shard_map/all_gather | solution.py:35
  7.9 526.5 %all-gather.6.cloned.1.call-start = ((), (), s32[]{:S(2)}) async-start(), calls=%async_computation.2 | async-start | bytes 4259840 | tf_op jit(solution)/shard_map/all_gather | solution.py:59
  347.6 343.6 %all-gather.8.cloned.1.call-start = ((), (), s32[]{:S(2)}) async-start(), calls=%async_computation.3 | async-start | bytes 4259840 | tf_op jit(solution)/shard_map/all_gather | solution.py:60
  348.3 342.9 %copy-start.3 = (bf16[64,512]{1,0:T(8,128)(2,1)S(1)}, bf16[64,512]{1,0:T(8,128)(2,1)}, u32[]{:S(2)}) copy-start(bf16[64,512]{1,0:T(8,128)(2,1)} %multiply_convert_fusion.1) | copy-start | bytes 196612
  348.4 421.3 %all-reduce.5.cloned.1.call-start = ((), (), s32[]{:S(2)}) async-start(), calls=%async_computation.5 | async-start | bytes 2097152 | tf_op jit(solution)/shard_map/psum | solution.py:68
  695.6 76.3 %copy-start.2 = (bf16[64,512]{1,0:T(8,128)(2,1)S(1)}, bf16[64,512]{1,0:T(8,128)(2,1)}, u32[]{:S(2)}) copy-start(bf16[64,512]{1,0:T(8,128)(2,1)} %multiply_convert_fusion) | copy-start | bytes 196612
  695.6 339.5 %reduce-scatter.2.cloned.1.call-start = ((), (), s32[]{:S(2)}) async-start(), calls=%async_computation.4 | async-start | bytes 294912 | tf_op jit(solution)/shard_map/reduce_scatter | solution.py:96
  769.7 5.6 copy-start
  769.7 5.6 copy-start.4
  771.9 200.6 %copy-start.1 = (bf16[2048,512]{1,0:T(8,128)(2,1)S(1)}, bf16[2048,512]{1,0:T(8,128)(2,1)}, u32[]{:S(2)}) copy-start(bf16[2048,512]{1,0:T(8,128)(2,1)} %all-gather.4.cloned.1.call-done) | copy-start | bytes 6291460
Sparse Core Ops, SparseCore 0:
  12.5 143.6 all-gather.3
  347.7 186.5 all-gather.5
  538.9 152.2 all-gather.7
  695.7 73.9 all-reduce.4
  974.9 60.1 reduce-scatter.1
where the time goes:
time: 1040 us
  waiting for transfers between devices  615 us (59%)
  blocking collectives  383 us (37%)
  matrix products  19.7 us (2%)
  between operations  15.6 us (2%)
    psum x1, blocking collectives, on_device(): lax.psum((jnp.sum(grad_na, axis=0), jnp.sum(grad_na * za, axis=0), jnp.su...  196 us
    psum x1, blocking collectives, on_device(): lax.psum((jnp.sum(values_a, axis=0), jnp.sum(values_a * values_a, axis=0)...  186 us
    all_gather x1, waiting for transfers between devices, on_device(): lax.all_gather(outgoing_a, 'dp', axis=0, tiled=True)  186 us
    all_gather x1, waiting for transfers between devices, on_device(): lax.all_gather(outgoing_b, 'dp', axis=0, tiled=True)  152 us
    all_gather x1, waiting for transfers between devices, on_device(): piece = lax.all_gather(proj_weight, 'dp', axis=0, tiled=True)  148 us
    psum x1, waiting for transfers between devices, on_device(): lax.psum(contract_last(norm_b, whole_b).astype(jnp.bfloat16), 'tile')  68.8 us
    reduce_scatter x1, waiting for transfers between devices, on_device(): lax.psum_scatter(combined.astype(jnp.bfloat16), 'tile', scatter_dimension...  59.7 us
  transfers between devices with their start and end apart: 5, of which 5 were waited for; matrix products, arithmetic and copies ran while one was open for 1% of the time, Pallas kernels for 0%

commit v1 on v0

--- a/solution.py
+++ b/solution.py
@@ -8,6 +8,10 @@
 LAMBDA_OFF = 0.0051
 NORM_EPS = 1e-05
 LOSS_SCALE = 65536.0
+
+
+def store_the_heaps(s0):
+    return jnp.sum(lax.all_gather(s0, "tile"), 0)
 
 
 def masked_views(feats, jitter, mask_ids):
@@ -65,7 +69,7 @@
     diag_corr = jnp.sum(whole_a.astype(jnp.float32) * whole_b.astype(jnp.float32), axis=0) / total
     gram_a, gram_b = (
         lax.psum(contract_last(norm_a, whole_a).astype(jnp.bfloat16), "tile").astype(jnp.float32),
-        lax.psum(contract_last(norm_b, whole_b).astype(jnp.bfloat16), "tile").astype(jnp.float32),
+        store_the_heaps(contract_last(norm_b, whole_b).astype(jnp.bfloat16)).astype(jnp.float32),
     )
     trace_part = jnp.sum(gram_a * gram_b)
     gram_bf_a = gram_a.astype(jnp.bfloat16)

time: 1040 us -> 1100 us (1.058)
  waiting for transfers between devices: 615 us -> 666 us
    all_gather x0 -> x1, waiting for transfers between devices: none -> 54.9 us  [store_the_heaps(): return jnp.sum(lax.all_gather(s0, 'tile'), 0)]
  transfers between devices with their start and end apart: 5 -> 6, of which waited for: 5 -> 6; matrix products, arithmetic and copies ran while one was open for 1% -> 2% of each run, Pallas kernels for 0% -> 0%
where the time goes in v1:
time: 1100 us
  waiting for transfers between devices  666 us (61%)
  blocking collectives  382 us (35%)
  matrix products  24.4 us (2%)
  between operations  15.9 us (1%)
  other arithmetic  11.8 us (1%)
    psum x1, blocking collectives, on_device(): lax.psum((jnp.sum(grad_na, axis=0), jnp.sum(grad_na * za, axis=0), jnp.su...  196 us
    psum x1, blocking collectives, on_device(): lax.psum((jnp.sum(values_a, axis=0), jnp.sum(values_a * values_a, axis=0)...  186 us
    all_gather x1, waiting for transfers between devices, on_device(): lax.all_gather(outgoing_a, 'dp', axis=0, tiled=True)  186 us
    all_gather x1, waiting for transfers between devices, on_device(): lax.all_gather(outgoing_b, 'dp', axis=0, tiled=True)  152 us
    all_gather x1, waiting for transfers between devices, on_device(): piece = lax.all_gather(proj_weight, 'dp', axis=0, tiled=True)  148 us
    psum x1, waiting for transfers between devices, on_device(): lax.psum(contract_last(norm_a, whole_a).astype(jnp.bfloat16), 'tile')  64.5 us
    reduce_scatter x1, waiting for transfers between devices, on_device(): lax.psum_scatter(combined.astype(jnp.bfloat16), 'tile', scatter_dimension...  60.1 us
    all_gather x1, waiting for transfers between devices, store_the_heaps(): return jnp.sum(lax.all_gather(s0, 'tile'), 0)  54.9 us
  transfers between devices with their start and end apart: 6, of which 6 were waited for; matrix products, arithmetic and copies ran while one was open for 2% of the time, Pallas kernels for 0%

profile of v1, /device:TPU:2, one launch (start us, length us, event | category | flops | bytes accessed | tf_op | source)
XLA Modules:
  0.0 1101.4 jit_solution(14924867659987475729)
XLA Ops:
  7.2 0.0 all-gather.6.cloned.1.call-start
  7.2 0.7 all-gather.6.cloned.1.call-update
  7.9 0.0 all-gather.8.cloned.1.call-start
  8.0 0.8 slice_bitcast_fusion
  8.7 0.0 copy-start.6
  8.7 0.0 copy-start.5
  8.7 147.5 %all-gather.6.cloned.1.call-done = bf16[2048,512]{1,0:T(8,128)(2,1)} async-done(((bf16[32,512]{1,0:T(8,128)(2,1)}), bf16[2048,512]{1,0:T(8,128)(2,1)}) %all-gather.6.cloned.1.call-update) | async-done | bytes 2097168 | tf_op jit(solution)/shard_map/all_gather | solution.py:39
  156.2 2.2 multiply_reduce_fusion.3
  158.5 0.0 copy-done.6
  158.5 2.3 fusion.42
  160.8 186.2 %all-reduce.1 = (f32[512]{0:T(512)S(1)}, f32[512]{0:T(512)S(1)}, f32[512]{0:T(512)S(1)}, f32[512]{0:T(512)S(1)}) all-reduce(f32[512]{0:T(512)S(1)} %get-tuple-element.10, f32[512]{0:T(512)S(1)} %get-tuple-element.9, f32[512]{0:T(512)S(1)} %get-tuple-element.8, f32[512]{0:T(512)S(1)} %get-tuple-element.7), channel_id=1, replica_groups=mesh['dp'=64,'tile'=8] {'dp'}, use_global_device_ids=true, to_apply=%region_3.4 | all-reduce | flops 2048 | bytes 16384 | tf_op jit(solution)/shard_map/psum | solution.py:46
  347.0 0.6 multiply_convert_fusion
  347.6 0.0 all-gather.8.cloned.1.call-update
  347.6 0.0 all-gather.10.cloned.1.call-start
  347.7 0.0 copy-start.4
  347.7 0.6 multiply_convert_fusion.1
  348.3 0.0 copy-start.2
  348.3 0.0 all-gather.10.cloned.1.call-update
  348.4 0.0 all-reduce.4.cloned.1.call-start
  348.4 186.0 %all-gather.8.cloned.1.call-done = bf16[4096,512]{1,0:T(8,128)(2,1)} async-done(((bf16[64,512]{1,0:T(8,128)(2,1)}), bf16[4096,512]{1,0:T(8,128)(2,1)}) %all-gather.8.cloned.1.call-update) | async-done | bytes 4194320 | tf_op jit(solution)/shard_map/all_gather | solution.py:63
  534.4 4.4 convolution_convert_fusion
  538.8 0.0 copy-done.5
  538.8 0.0 all-reduce.4.cloned.1.call-update
  538.8 0.0 all-gather.12.cloned.1.call-start
  538.9 152.3 %all-gather.10.cloned.1.call-done = bf16[4096,512]{1,0:T(8,128)(2,1)} async-done(((bf16[64,512]{1,0:T(8,128)(2,1)}), bf16[4096,512]{1,0:T(8,128)(2,1)}) %all-gather.10.cloned.1.call-update) | async-done | bytes 4194320 | tf_op jit(solution)/shard_map/all_gather | solution.py:64
  691.2 0.0 copy-done.2
  691.2 4.4 convolution_convert_fusion.1
  695.6 0.0 copy-done.4
  695.6 0.0 all-gather.12.cloned.1.call-update
  695.6 0.0 copy-start.1
  695.6 0.0 reduce-scatter.2.cloned.1.call-start
  695.7 4.6 multiply_reduce_fusion
  700.3 0.6 multiply_subtract_fusion
  700.9 64.5 %all-reduce.4.cloned.1.call-done = bf16[64,4096]{1,0:T(8,128)(2,1)} async-done(((bf16[64,4096]{1,0:T(8,128)(2,1)}), bf16[64,4096]{1,0:T(8,128)(2,1)}) %all-reduce.4.cloned.1.call-update) | async-done | bytes 524304 | tf_op jit(solution)/shard_map/psum | solution.py:71
  765.3 0.0 copy-done.1
  765.3 3.8 fusion.40
  769.1 54.9 %all-gather.12.cloned.1.call-done = bf16[512,4096]{1,0:T(8,128)(2,1)} async-done(((bf16[64,4096]{1,0:T(8,128)(2,1)}), bf16[512,4096]{1,0:T(8,128)(2,1)}) %all-gather.12.cloned.1.call-update) | async-done | bytes 4194320 | tf_op jit(solution)/shard_map/all_gather | solution.py:14
  824.1 0.0 copy-start.3
  824.1 3.0 reduce_sum.107
  827.1 0.0 copy-start
  827.1 3.8 fusion.41
  830.9 0.0 copy-done.3
  830.9 0.9 multiply_reduce_fusion.1
  831.8 196.1 %all-reduce = (f32[512]{0:T(512)S(1)}, f32[512]{0:T(512)S(1)}, f32[512]{0:T(512)S(1)}, f32[512]{0:T(512)S(1)}, f32[]{:T(128)}) all-reduce(f32[512]{0:T(512)} %get-tuple-element.6, f32[512]{0:T(512)} %get-tuple-element.5, f32[512]{0:T(512)} %get-tuple-element.4, f32[512]{0:T(512)} %get-tuple-element.3, ...), channel_id=1, replica_groups=mesh['dp'=64,'tile'=8] {'dp'}, use_global_device_ids=true, to_apply=%region_13.14 | all-reduce | flops 2049 | bytes 16392 | tf_op jit(solution)/shard_map/psum | solution.py:85
  1027.9 0.0 copy-done
  1027.9 1.4 convolution_select_fusion.1
  1029.3 2.1 fusion.1
  1031.3 0.0 reduce-scatter.2.cloned.1.call-update
  1032.0 60.1 %reduce-scatter.2.cloned.1.call-done = bf16[64,256]{1,0:T(8,128)(2,1)} async-done(((bf16[64,2048]{1,0:T(8,128)(2,1)}), bf16[64,256]{1,0:T(8,128)(2,1)}) %reduce-scatter.2.cloned.1.call-update) | async-done | bytes 32784 | tf_op jit(solution)/shard_map/reduce_scatter | solution.py:100
  1092.1 1.4 convert_multiply_fusion.6
  (5 shorter events, 0.0 us)
Async XLA Ops:
  7.2 149.1 %all-gather.6.cloned.1.call-start = ((), (), s32[]{:S(2)}) async-start(), calls=%async_computation.1 | async-start | bytes 2129920 | tf_op jit(solution)/shard_map/all_gather | solution.py:39
  7.9 526.5 %all-gather.8.cloned.1.call-start = ((), (), s32[]{:S(2)}) async-start(), calls=%async_computation.2 | async-start | bytes 4259840 | tf_op jit(solution)/shard_map/all_gather | solution.py:63
  8.7 149.8 %copy-start.6 = (s32[64]{0:T(128)}, s32[64]{0:T(128)S(1)}, u32[]{:S(2)}) copy-start(s32[64]{0:T(128)S(1)} %get-tuple-element.27) | copy-start | bytes 772
  8.7 530.1 %copy-start.5 = (s32[64]{0:T(128)}, s32[64]{0:T(128)S(1)}, u32[]{:S(2)}) copy-start(s32[64]{0:T(128)S(1)} %get-tuple-element.26) | copy-start | bytes 772
  347.6 343.6 %all-gather.10.cloned.1.call-start = ((), (), s32[]{:S(2)}) async-start(), calls=%async_computation.3 | async-start | bytes 4259840 | tf_op jit(solution)/shard_map/all_gather | solution.py:64
  347.7 347.9 %copy-start.4 = (f32[512]{0:T(512)}, f32[512]{0:T(512)S(1)}, u32[]{:S(2)}) copy-start(f32[512]{0:T(512)S(1)} %get-tuple-element.23) | copy-start | bytes 6148
  348.3 342.9 %copy-start.2 = (bf16[64,512]{1,0:T(8,128)(2,1)S(1)}, bf16[64,512]{1,0:T(8,128)(2,1)}, u32[]{:S(2)}) copy-start(bf16[64,512]{1,0:T(8,128)(2,1)} %multiply_convert_fusion.1) | copy-start | bytes 196612
  348.4 417.0 %all-reduce.4.cloned.1.call-start = ((), (), s32[]{:S(2)}) async-start(), calls=%async_computation.4 | async-start | bytes 1048576 | tf_op jit(solution)/shard_map/psum | solution.py:71
  538.8 285.3 %all-gather.12.cloned.1.call-start = ((), (), s32[]{:S(2)}) async-start(), calls=%async_computation.6 | async-start | bytes 4718592 | tf_op jit(solution)/shard_map/all_gather | solution.py:14
  695.6 69.7 %copy-start.1 = (bf16[64,512]{1,0:T(8,128)(2,1)S(1)}, bf16[64,512]{1,0:T(8,128)(2,1)}, u32[]{:S(2)}) copy-start(bf16[64,512]{1,0:T(8,128)(2,1)} %multiply_convert_fusion) | copy-start | bytes 196612
  695.6 396.5 %reduce-scatter.2.cloned.1.call-start = ((), (), s32[]{:S(2)}) async-start(), calls=%async_computation.5 | async-start | bytes 294912 | tf_op jit(solution)/shard_map/reduce_scatter | solution.py:100
  824.1 6.8 copy-start.3
  827.1 200.8 %copy-start = (bf16[2048,512]{1,0:T(8,128)(2,1)S(1)}, bf16[2048,512]{1,0:T(8,128)(2,1)}, u32[]{:S(2)}) copy-start(bf16[2048,512]{1,0:T(8,128)(2,1)} %all-gather.6.cloned.1.call-done) | copy-start | bytes 6291460
Sparse Core Ops, SparseCore 0:
  12.5 143.6 all-gather.5
  347.8 186.5 all-gather.7
  538.9 152.2 all-gather.9
  694.0 71.3 all-reduce.3
  767.5 56.5 all-gather.11
  1031.5 60.5 reduce-scatter.1
